TPU v7x, 256 devices: a whole 4x4x8 slice. The times are simulated.
256 devices in a mesh: seq: 128 (over y, z, x), head: 2 (over core).
Axes of the slice: x: 4, y: 4, z: 8, core: 2. Of those that a mesh axis runs over, the one named last changes fastest.
Arguments:
- queries: bfloat16 [8192, 1536], P('seq', 'head'), may hold values from -6 to 6
- key_vectors: bfloat16 [8192, 512], P('seq', 'head'), may hold values from -6 to 6
- value_vectors: bfloat16 [8192, 512], P('seq', 'head'), may hold values from -6 to 6
- lengths: int32 [64], replicated, may hold values from 1 to 256, 8192 in all
- out_weight: bfloat16 [1536, 1536], P('head', 'seq'), may hold values from -0.15625 to 0.15625
- residual: bfloat16 [8192, 1536], P(('seq', 'head')), may hold values from -6 to 6
- norm_gain: float32 [1536], replicated, may hold values from 0.1 to 1.9
- route_ids: int32 [8192, 6], P(('seq', 'head')), may hold values from 0 to 63, all different within a row; in each aligned block of 32 rows (0 to 31, 32 to 63, ...) at most 6 rows name the same one
- route_logits: float32 [8192, 6], P(('seq', 'head')), may hold values from -8 to 340
- shared_gate_up: bfloat16 [1536, 2, 1024], P(None, None, ('seq', 'head')), may hold values from -0.15625 to 0.15625
- shared_down: bfloat16 [1024, 1536], P(('seq', 'head')), may hold values from -0.1875 to 0.1875
- expert_gate_up: bfloat16 [128, 1536, 2, 256], P('seq'), may hold values from -0.15625 to 0.15625
- expert_down: bfloat16 [128, 256, 1536], P('seq'), may hold values from -0.25 to 0.25
- cache_blocks: bfloat16 [128, 128, 8, 4, 128], P('seq', None, None, 'head'), may hold values from -6 to 6
- block_table: int32 [128], replicated, may hold values from 0 to 127, each once
Outputs:
- layer_out: bfloat16 [8192, 1536], P(('seq', 'head'))
- cache_out: bfloat16 [128, 128, 8, 4, 128], P(None, 'seq', None, 'head')
Inputs may be any that keep to these rules, and one draw needn't show every extreme that they name: The lengths sum to 8192. `route_ids`: each token names 6 different experts; among the tokens of one device no expert is named more than 6 times. `block_table`: every block appears once.
All inputs are finite; a program needn't handle non-finite values.
Results may differ from a plain program's by a relative error of at most 0.0095.
Values may be sent and summed in bfloat16 or wider, within the bound.
A program may use at most 64 MiB of HBM per device.

v0:
```python
import math
import jax
import jax.numpy as jnp
from jax import lax
from jax.sharding import PartitionSpec as P

HD = 128
EXPERTS = 64
TOP = 6
REACH = 4
HALVES = 128
CAP = 6
NEGATIVE = -1e30
EPSILON = 1e-05


def from_behind(shard, axis, by):
    devices = lax.axis_size(axis)
    pairs = [(i, i + by) for i in range(devices) if 0 <= i + by < devices]
    return lax.ppermute(shard, axis, pairs)


def segment_of(positions, lengths):
    request_ends = jnp.cumsum(lengths)
    passed = (request_ends[None, :] <= positions[:, None]).astype(jnp.int32)
    return jnp.sum(passed, axis=1)


def shared_ffn(rows_in, gate_up_part, down_part):
    shared_both = jnp.einsum(
        "td,dcf->tcf", rows_in, gate_up_part, preferred_element_type=jnp.float32
    )
    shared_act = (jax.nn.silu(shared_both[:, 0]) * shared_both[:, 1]).astype(jnp.bfloat16)
    return jnp.dot(shared_act, down_part, preferred_element_type=jnp.float32)


def shards(
    queries,
    key_vectors,
    value_vectors,
    lengths,
    out_weight,
    residual,
    norm_gain,
    route_ids,
    route_logits,
    shared_gate_up,
    shared_down,
    expert_gate_up,
    expert_down,
    cache_blocks,
    block_table,
):
    handed = lax.all_to_all(cache_blocks, "seq", split_axis=1, concat_axis=0, tiled=True)
    cache_out = jnp.take(handed, block_table, axis=0)
    tok_rows = queries.shape[0]
    seq_index = lax.axis_index("seq")
    earlier = [
        from_behind((key_vectors, value_vectors), "seq", offset) for offset in range(REACH, 0, -1)
    ]
    window_keys = jnp.concatenate([member[0] for member in earlier] + [key_vectors], axis=0)
    window_values = jnp.concatenate([member[1] for member in earlier] + [value_vectors], axis=0)
    key_count = window_keys.shape[0]
    kv_heads = key_vectors.shape[1] // HD
    query_heads = queries.shape[1] // HD
    group_size = query_heads // kv_heads
    query_pos = seq_index * tok_rows + jnp.arange(tok_rows, dtype=jnp.int32)
    key_pos = (seq_index - REACH) * tok_rows + jnp.arange(key_count, dtype=jnp.int32)
    visible = (key_pos[None, :] >= 0) & (key_pos[None, :] <= query_pos[:, None])
    visible = visible & (
        segment_of(key_pos, lengths)[None, :] == segment_of(query_pos, lengths)[:, None]
    )
    query_part = queries.reshape(tok_rows, kv_heads, group_size, HD)
    key_part = window_keys.reshape(key_count, kv_heads, HD)
    value_part = window_values.reshape(key_count, kv_heads, HD)
    scores = jnp.einsum(
        "tkgd,wkd->kgtw", query_part, key_part, preferred_element_type=jnp.float32
    ) * (1.0 / math.sqrt(HD))
    scores = jnp.where(visible[None, None], scores, NEGATIVE)
    row_max = jnp.max(scores, axis=-1, keepdims=True)
    weights = jnp.exp(scores - row_max)
    row_total = jnp.sum(weights, axis=-1)
    weighted = jnp.einsum(
        "kgtw,wkd->tkgd",
        weights.astype(jnp.bfloat16),
        value_part,
        preferred_element_type=jnp.float32,
    )
    heads = (weighted / jnp.transpose(row_total, (2, 0, 1))[..., None]).astype(jnp.bfloat16)
    heads = heads.reshape(tok_rows, query_heads * HD)
    partial_out = jnp.dot(
        heads,
        lax.all_gather(out_weight, "seq", axis=1, tiled=True),
        preferred_element_type=jnp.float32,
    )
    attn_out = lax.psum_scatter(partial_out, "head", scatter_dimension=0, tiled=True)
    mixed = residual.astype(jnp.float32) + attn_out
    mean_square = jnp.mean(mixed * mixed, axis=-1, keepdims=True)
    normed = (mixed * lax.rsqrt(mean_square + EPSILON) * norm_gain).astype(jnp.bfloat16)
    gate_up_all, down_all = (
        lax.all_gather(shared_gate_up, ("seq", "head"), axis=2, tiled=True),
        lax.all_gather(shared_down, ("seq", "head"), axis=0, tiled=True),
    )
    shared_part = shared_ffn(normed, gate_up_all, down_all)
    own_tokens = normed.shape[0]
    width_model = normed.shape[1]
    flat_ids = route_ids.reshape(-1)
    onehot = (flat_ids[:, None] == jnp.arange(EXPERTS, dtype=jnp.int32)[None, :]).astype(jnp.int32)
    slot_rank = jnp.sum((jnp.cumsum(onehot, axis=0) - 1) * onehot, axis=1)
    first_slot = flat_ids * CAP + slot_rank
    second_slot = (flat_ids + EXPERTS) * CAP + slot_rank
    token_of = jnp.arange(flat_ids.shape[0], dtype=jnp.int32) // TOP
    routed_rows = normed[token_of]
    outgoing = jnp.zeros((HALVES * CAP, width_model), jnp.bfloat16)
    outgoing = outgoing.at[jnp.concatenate([first_slot, second_slot])].set(
        jnp.concatenate([routed_rows, routed_rows], axis=0)
    )
    local_halves = expert_gate_up.shape[0]
    outgoing = outgoing.reshape(HALVES // local_halves, local_halves, CAP, width_model)
    gate_up = jnp.einsum(
        "nsjd,sdcf->nsjcf",
        lax.all_to_all(outgoing, "seq", split_axis=0, concat_axis=0, tiled=True),
        expert_gate_up,
        preferred_element_type=jnp.float32,
    )
    expert_act = (jax.nn.silu(gate_up[:, :, :, 0]) * gate_up[:, :, :, 1]).astype(jnp.bfloat16)
    half_out = jnp.einsum(
        "nsjf,sfd->nsjd", expert_act, expert_down, preferred_element_type=jnp.float32
    ).astype(jnp.bfloat16)
    returned = lax.all_to_all(half_out, "seq", split_axis=0, concat_axis=0, tiled=True)
    returned = returned.reshape(HALVES * CAP, width_model)
    pair_sum = returned[first_slot].astype(jnp.float32) + returned[second_slot].astype(jnp.float32)
    route_probs = jax.nn.softmax(route_logits, axis=-1)
    routed = jnp.sum(
        route_probs[:, :, None] * pair_sum.reshape(own_tokens, TOP, width_model), axis=1
    )
    layer_out = (mixed + shared_part + routed).astype(jnp.bfloat16)
    return (layer_out, cache_out)


def solution(mesh):
    in_specs = (
        P("seq", "head"),
        P("seq", "head"),
        P("seq", "head"),
        P(),
        P("head", "seq"),
        P(("seq", "head"), None),
        P(),
        P(("seq", "head"), None),
        P(("seq", "head"), None),
        P(None, None, ("seq", "head")),
        P(("seq", "head"), None),
        P("seq", None, None, None),
        P("seq", None, None),
        P("seq", None, None, "head", None),
        P(),
    )
    out_specs = (P(("seq", "head"), None), P(None, "seq", None, "head", None))
    return jax.shard_map(shards, mesh=mesh, in_specs=in_specs, out_specs=out_specs, check_vma=False)
```

profile of v0, /device:TPU:1, one launch (start us, length us, event | category | flops | bytes accessed | tf_op | source)
XLA Modules:
  0.0 410.7 jit_solution(4338545764262982124)
XLA Ops:
  8.8 4.4 %collective-permute-start.4 = (bf16[64,256]{1,0:T(8,128)(2,1)}, bf16[64,256]{1,0:T(8,128)(2,1)S(1)}, u32[]{:S(2)}, u32[]{:S(2)}) collective-permute-start(bf16[64,256]{1,0:T(8,128)(2,1)} %param.16), channel_id=1, source_target_pairs={{0,8},{2,10},{4,12},{6,14},{8,16},{10,18},{12,20},{14,22},{16,24},... | collective-permute-start | bytes 98312 | tf_op jit(solution)/shard_map/ppermute | solution.py:20
  13.2 4.4 %collective-permute-start.5 = (bf16[64,256]{1,0:T(8,128)(2,1)}, bf16[64,256]{1,0:T(8,128)(2,1)S(1)}, u32[]{:S(2)}, u32[]{:S(2)}) collective-permute-start(bf16[64,256]{1,0:T(8,128)(2,1)} %param.16), channel_id=1, source_target_pairs={{0,6},{2,8},{4,10},{6,12},{8,14},{10,16},{12,18},{14,20},{16,22},{... | collective-permute-start | bytes 98312 | tf_op jit(solution)/shard_map/ppermute | solution.py:20
  17.6 3.8 collective-permute-start.6
  21.4 2.5 collective-permute-start.7
  23.9 3.6 collective-permute-start
  29.8 6.5 %collective-permute-start.1 = (bf16[64,256]{1,0:T(8,128)(2,1)}, bf16[64,256]{1,0:T(8,128)(2,1)S(1)}, u32[]{:S(2)}, u32[]{:S(2)}) collective-permute-start(bf16[64,256]{1,0:T(8,128)(2,1)} %param.17), channel_id=1, source_target_pairs={{0,6},{2,8},{4,10},{6,12},{8,14},{10,16},{12,18},{14,20},{16,22},{... | collective-permute-start | bytes 98312 | tf_op jit(solution)/shard_map/ppermute | solution.py:20
  36.4 3.1 collective-permute-start.2
  44.1 83.4 %all-gather.8.cloned.1.call-done = bf16[128,12,768]{2,1,0:T(8,128)(2,1)} async-done(((bf16[1,12,768]{2,1,0:T(8,128)(2,1)}), bf16[128,12,768]{2,1,0:T(8,128)(2,1)}) %all-gather.8.cloned.1.call-update) | async-done | bytes 2359312 | tf_op jit(solution)/shard_map/all_gather | solution.py:93
  127.5 3.6 reshape.454
  135.4 12.7 %reduce-scatter.2.cloned.1.call-done = f32[32,1536]{1,0:T(8,128)} async-done(((f32[64,1536]{1,0:T(8,128)}), f32[32,1536]{1,0:T(8,128)}) %reduce-scatter.2.cloned.1.call-update) | async-done | bytes 196624 | tf_op jit(solution)/shard_map/reduce_scatter | solution.py:96
  150.2 1.9 gather_fusion
  152.1 3.9 scatter_custom_fusion
  156.0 2.5 reshape.403
  158.5 89.1 %all_to_all.22 = bf16[128,1,6,1536]{3,2,1,0:T(8,128)(2,1)} all-to-all(bf16[128,1,6,1536]{3,2,1,0:T(8,128)(2,1)} %bitcast.96), channel_id=1, replica_groups=mesh['seq'=128,'head'=2] {'seq'}, dimensions={0} | all-to-all | bytes 4718592 | tf_op jit(solution)/shard_map/all_to_all | solution.py:122
  247.6 10.7 %all-to-all-start.2 = ((bf16[1,128,8,2,128]{4,3,2,0,1:T(2,128)(2,1)}), bf16[1,128,8,2,128]{4,3,2,0,1:T(2,128)(2,1)S(1)}, u32[]{:S(2)}, u32[]{:S(2)}) async-start(bf16[1,128,8,2,128]{4,3,2,0,1:T(2,128)(2,1)} %bitcast.36), calls=%async_computation.3 | async-start | bytes 1048576 | tf_op jit(solution)/shard_map/all_to_all | solution.py:54
  258.3 3.3 fusion.10
  262.4 3.0 copy.68
  265.3 9.3 %all-to-all-done.2 = bf16[1,128,8,2,128]{4,3,2,0,1:T(2,128)(2,1)S(1)} async-done(((bf16[1,128,8,2,128]{4,3,2,0,1:T(2,128)(2,1)}), bf16[1,128,8,2,128]{4,3,2,0,1:T(2,128)(2,1)S(1)}, u32[]{:S(2)}, u32[]{:S(2)}) %all-to-all-start.2) | async-done | bytes 524320 | tf_op jit(solution)/shard_map/all_to_all | solution.py:54
  274.6 8.9 %all-to-all-start.1 = ((bf16[128,1,6,1536]{3,2,1,0:T(8,128)(2,1)}), bf16[128,1,6,1536]{3,2,1,0:T(8,128)(2,1)}, u32[]{:S(2)}, u32[]{:S(2)}) async-start(bf16[128,1,6,1536]{3,2,1,0:T(8,128)(2,1)} %copy.68), calls=%async_computation.2 | async-start | bytes 6291456 | tf_op jit(solution)/shard_map/all_to_all | solution.py:130
  287.2 5.9 %reshape.456 = bf16[1024,1536]{1,0:T(8,128)(2,1)} reshape(bf16[256,4,1536]{2,1,0:T(4,128)(2,1)} %all-gather.10.cloned.1.call-done) | data formatting | bytes 6291456
  293.1 91.6 %all-gather.6.cloned.1.call-done = bf16[1536,2,1024]{0,1,2:T(2,128)(2,1)} async-done(((bf16[1536,2,4]{0,1,2:T(2,128)(2,1)}), bf16[1536,2,1024]{0,1,2:T(2,128)(2,1)}) %all-gather.6.cloned.1.call-update) | async-done | bytes 6291472 | tf_op jit(solution)/shard_map/all_gather | solution.py:101
  384.8 5.5 %fusion = f32[32,2,1024]{2,0,1:T(8,128)} fusion(bf16[1536,2,1024]{0,1,2:T(2,128)(2,1)} %all-gather.6.cloned.1.call-done, bf16[32,1536]{1,0:T(8,128)(2,1)S(1)} %multiply_convert_fusion), kind=kOutput, calls=%fused_computation.5 | convolution fusion | flops 201326592 | bytes 6651904 | tf_op jit(solution)/shard_map/td,dcf->tcf/dot_general | solution.py:30
  390.2 3.7 reshape.407
  399.8 3.4 fusion.7
  (103 shorter events, 24.0 us)
Async XLA Ops:
  8.0 253.6 %copy-start = (bf16[1,256,1536]{2,1,0:T(8,128)(2,1)S(1)}, bf16[1,256,1536]{2,1,0:T(8,128)(2,1)}, u32[]{:S(2)}) copy-start(bf16[1,256,1536]{2,1,0:T(8,128)(2,1)} %param.27) | copy-start | bytes 2359300
  8.0 119.5 %all-gather.8.cloned.1.call-start = ((), (), s32[]{:S(2)}) async-start(), calls=%async_computation.6 | async-start | bytes 3170304 | tf_op jit(solution)/shard_map/all_gather | solution.py:93
  8.7 139.4 %reduce-scatter.2.cloned.1.call-start = ((), (), s32[]{:S(2)}) async-start(), calls=%async_computation.4 | async-start | bytes 589824 | tf_op jit(solution)/shard_map/reduce_scatter | solution.py:96
  8.8 21.0 %collective-permute-start.4 = (bf16[64,256]{1,0:T(8,128)(2,1)}, bf16[64,256]{1,0:T(8,128)(2,1)S(1)}, u32[]{:S(2)}, u32[]{:S(2)}) collective-permute-start(bf16[64,256]{1,0:T(8,128)(2,1)} %param.16), channel_id=1, source_target_pairs={{0,8},{2,10},{4,12},{6,14},{8,16},{10,18},{12,20},{14,22},{16,24},... | collective-permute-start | bytes 98312 | tf_op jit(solution)/shard_map/ppermute | solution.py:20
  13.2 23.2 %collective-permute-start.5 = (bf16[64,256]{1,0:T(8,128)(2,1)}, bf16[64,256]{1,0:T(8,128)(2,1)S(1)}, u32[]{:S(2)}, u32[]{:S(2)}) collective-permute-start(bf16[64,256]{1,0:T(8,128)(2,1)} %param.16), channel_id=1, source_target_pairs={{0,6},{2,8},{4,10},{6,12},{8,14},{10,16},{12,18},{14,20},{16,22},{... | collective-permute-start | bytes 98312 | tf_op jit(solution)/shard_map/ppermute | solution.py:20
  17.6 22.0 %collective-permute-start.6 = (bf16[64,256]{1,0:T(8,128)(2,1)}, bf16[64,256]{1,0:T(8,128)(2,1)S(1)}, u32[]{:S(2)}, u32[]{:S(2)}) collective-permute-start(bf16[64,256]{1,0:T(8,128)(2,1)} %param.16), channel_id=1, source_target_pairs={{0,4},{2,6},{4,8},{6,10},{8,12},{10,14},{12,16},{14,18},{16,20},{1... | collective-permute-start | bytes 98312 | tf_op jit(solution)/shard_map/ppermute | solution.py:20
  21.4 19.5 %collective-permute-start.7 = (bf16[64,256]{1,0:T(8,128)(2,1)}, bf16[64,256]{1,0:T(8,128)(2,1)S(1)}, u32[]{:S(2)}, u32[]{:S(2)}) collective-permute-start(bf16[64,256]{1,0:T(8,128)(2,1)} %param.16), channel_id=1, source_target_pairs={{0,2},{2,4},{4,6},{6,8},{8,10},{10,12},{12,14},{14,16},{16,18},{18... | collective-permute-start | bytes 98312 | tf_op jit(solution)/shard_map/ppermute | solution.py:20
  23.9 17.8 %collective-permute-start = (bf16[64,256]{1,0:T(8,128)(2,1)}, bf16[64,256]{1,0:T(8,128)(2,1)S(1)}, u32[]{:S(2)}, u32[]{:S(2)}) collective-permute-start(bf16[64,256]{1,0:T(8,128)(2,1)} %param.17), channel_id=1, source_target_pairs={{0,8},{2,10},{4,12},{6,14},{8,16},{10,18},{12,20},{14,22},{16,24},... | collective-permute-start | bytes 98312 | tf_op jit(solution)/shard_map/ppermute | solution.py:20
  29.8 11.9 %collective-permute-start.1 = (bf16[64,256]{1,0:T(8,128)(2,1)}, bf16[64,256]{1,0:T(8,128)(2,1)S(1)}, u32[]{:S(2)}, u32[]{:S(2)}) collective-permute-start(bf16[64,256]{1,0:T(8,128)(2,1)} %param.17), channel_id=1, source_target_pairs={{0,6},{2,8},{4,10},{6,12},{8,14},{10,16},{12,18},{14,20},{16,22},{... | collective-permute-start | bytes 98312 | tf_op jit(solution)/shard_map/ppermute | solution.py:20
  36.4 5.4 %collective-permute-start.2 = (bf16[64,256]{1,0:T(8,128)(2,1)}, bf16[64,256]{1,0:T(8,128)(2,1)S(1)}, u32[]{:S(2)}, u32[]{:S(2)}) collective-permute-start(bf16[64,256]{1,0:T(8,128)(2,1)} %param.17), channel_id=1, source_target_pairs={{0,4},{2,6},{4,8},{6,10},{8,12},{10,14},{12,16},{14,18},{16,20},{1... | collective-permute-start | bytes 98312 | tf_op jit(solution)/shard_map/ppermute | solution.py:20
  39.5 2.7 collective-permute-start.3
  131.1 2.3 copy-start.3
  131.1 2.9 copy-start.4
  131.2 16.9 %copy-start.1 = (bf16[32,1536]{1,0:T(8,128)(2,1)S(1)}, bf16[32,1536]{1,0:T(8,128)(2,1)}, u32[]{:S(2)}) copy-start(bf16[32,1536]{1,0:T(8,128)(2,1)} %param.20) | copy-start | bytes 294916
  131.2 18.0 %copy-start.5 = (f32[1536]{0:T(1024)S(1)}, f32[1536]{0:T(1024)}, u32[]{:S(2)}) copy-start(f32[1536]{0:T(1024)} %param.21) | copy-start | bytes 18436
  132.8 154.4 %all-gather.10.cloned.1.call-start = ((), (), s32[]{:S(2)}) async-start(), calls=%async_computation.7 | async-start | bytes 3158016 | tf_op jit(solution)/shard_map/all_gather | solution.py:102
  133.4 251.4 %all-gather.6.cloned.1.call-start = ((), (), s32[]{:S(2)}) async-start(), calls=%async_computation.5 | async-start | bytes 6316032 | tf_op jit(solution)/shard_map/all_gather | solution.py:101
  158.5 99.8 %copy-start.6 = (bf16[1,1536,2,256]{3,2,1,0:T(2,128)(2,1)S(1)}, bf16[1,1536,2,256]{3,2,1,0:T(2,128)(2,1)}, u32[]{:S(2)}) copy-start(bf16[1,1536,2,256]{3,2,1,0:T(2,128)(2,1)} %param.26) | copy-start | bytes 4718596
  247.6 27.1 %all-to-all-start.2 = ((bf16[1,128,8,2,128]{4,3,2,0,1:T(2,128)(2,1)}), bf16[1,128,8,2,128]{4,3,2,0,1:T(2,128)(2,1)S(1)}, u32[]{:S(2)}, u32[]{:S(2)}) async-start(bf16[1,128,8,2,128]{4,3,2,0,1:T(2,128)(2,1)} %bitcast.36), calls=%async_computation.3 | async-start | bytes 1048576 | tf_op jit(solution)/shard_map/all_to_all | solution.py:54
  265.3 18.6 %copy-start.2 = (f32[32,6]{0,1:T(8,128)S(1)}, f32[32,6]{0,1:T(8,128)}, u32[]{:S(2)}) copy-start(f32[32,6]{0,1:T(8,128)} %param.23) | copy-start | bytes 2308
  265.3 18.8 %copy-start.7 = (s32[128]{0:T(128)S(1)}, s32[128]{0:T(128)}, u32[]{:S(2)}) copy-start(s32[128]{0:T(128)} %param.29) | copy-start | bytes 1540
  274.6 115.6 %all-to-all-start.1 = ((bf16[128,1,6,1536]{3,2,1,0:T(8,128)(2,1)}), bf16[128,1,6,1536]{3,2,1,0:T(8,128)(2,1)}, u32[]{:S(2)}, u32[]{:S(2)}) async-start(bf16[128,1,6,1536]{3,2,1,0:T(8,128)(2,1)} %copy.68), calls=%async_computation.2 | async-start | bytes 6291456 | tf_op jit(solution)/shard_map/all_to_all | solution.py:130
Sparse Core Ops, SparseCore 0:
  12.5 114.9 all-gather.7
  132.9 15.1 reduce-scatter.1
Sparse Core Ops, SparseCore 1:
  137.6 121.0 all-gather.9
  263.6 121.1 all-gather.5
where the time goes:
time: 412 us; the launch traced here: 411 us
  waiting for transfers between devices  199 us (48%)
  blocking collectives  89.1 us (22%)
  starting transfers between devices  49.4 us (12%)
  local copies, waits for them, and re-layouts  31.2 us (8%)
  between operations  16 us (4%)
  matrix products  15.2 us (4%)
  other arithmetic  11.1 us (3%)
    all_gather x1, waiting for transfers between devices, shards(): lax.all_gather(shared_gate_up, ('seq', 'head'), axis=2, tiled=True)  91.6 us
    all_to_all x1, blocking collectives, shards(): lax.all_to_all(outgoing, 'seq', split_axis=0, concat_axis=0, tiled=True)  89.1 us
    all_gather x1, waiting for transfers between devices, shards(): lax.all_gather(out_weight, 'seq', axis=1, tiled=True)  83.4 us
    ppermute x8, starting transfers between devices, from_behind(): return lax.ppermute(shard, axis, pairs)  29.7 us
    reduce_scatter x1, waiting for transfers between devices, shards(): lax.psum_scatter(partial_out, 'head', scatter_dimension=0, tiled=True)  12.7 us
    all_to_all x1, starting transfers between devices, shards(): lax.all_to_all(cache_blocks, 'seq', split_axis=1, concat_axis=0, tiled=True)  10.7 us
    unnamed x28, local copies, waits for them, and re-layouts  10.3 us
    all_to_all x1, waiting for transfers between devices, shards(): lax.all_to_all(cache_blocks, 'seq', split_axis=1, concat_axis=0, tiled=True)  9.29 us
  transfers between devices with their start and end apart: 14, of which 5 were waited for; matrix products, arithmetic and copies ran while one was open for 10% of the time, Pallas kernels for 0%

commit v1 on v0

--- a/solution.py
+++ b/solution.py
@@ -12,6 +12,19 @@
 CAP = 6
 NEGATIVE = -1e30
 EPSILON = 1e-05
+
+
+def _lay_thing(u_in, dim_k):
+    clean = jnp.concatenate(
+        lax.all_to_all(
+            jnp.stack([u_in for _ in range(lax.axis_size("seq"))], axis=0),
+            "seq",
+            concat_axis=0,
+            split_axis=0,
+        ),
+        axis=dim_k,
+    )
+    return clean
 
 
 def from_behind(shard, axis, by):
@@ -88,11 +101,7 @@
     )
     heads = (weighted / jnp.transpose(row_total, (2, 0, 1))[..., None]).astype(jnp.bfloat16)
     heads = heads.reshape(tok_rows, query_heads * HD)
-    partial_out = jnp.dot(
-        heads,
-        lax.all_gather(out_weight, "seq", axis=1, tiled=True),
-        preferred_element_type=jnp.float32,
-    )
+    partial_out = jnp.dot(heads, _lay_thing(out_weight, 1), preferred_element_type=jnp.float32)
     attn_out = lax.psum_scatter(partial_out, "head", scatter_dimension=0, tiled=True)
     mixed = residual.astype(jnp.float32) + attn_out
     mean_square = jnp.mean(mixed * mixed, axis=-1, keepdims=True)

time: 412 us -> 397 us (0.964)
  waiting for transfers between devices: 199 us -> 170 us
  starting transfers between devices: 49.4 us -> 63.4 us
    all_gather x1 -> x0, waiting for transfers between devices: 83.4 us -> none  [shards(): lax.all_gather(out_weight, 'seq', axis=1, tiled=True)]
    ppermute x8, waiting for transfers between devices: 0.44 us -> 48.7 us  [from_behind(): return lax.ppermute(shard, axis, pairs)]
    all_to_all x0 -> x1, starting transfers between devices: none -> 16.9 us  [_lay_thing(): lax.all_to_all(jnp.stack([u_in for _ in range(lax.axis_size('seq'))], axi...]
    reduce_scatter x1, waiting for transfers between devices: 12.7 us -> 19.6 us  [shards(): lax.psum_scatter(partial_out, 'head', scatter_dimension=0, tiled=True)]
    unnamed x28 -> x35, local copies, waits for them, and re-layouts: 10.3 us -> 6.72 us
  transfers between devices with their start and end apart: 14 -> 14, of which waited for: 5 -> 5; matrix products, arithmetic and copies ran while one was open for 10% -> 9% of each run, Pallas kernels for 0% -> 0%
where the time goes in v1:
time: 397 us; the launch traced here: 395 us
  waiting for transfers between devices  170 us (43%)
  blocking collectives  89.1 us (22%)
  starting transfers between devices  63.4 us (16%)
  local copies, waits for them, and re-layouts  30.8 us (8%)
  between operations  16.1 us (4%)
  matrix products  15.2 us (4%)
  other arithmetic  11.1 us (3%)
    all_gather x1, waiting for transfers between devices, shards(): lax.all_gather(shared_gate_up, ('seq', 'head'), axis=2, tiled=True)  91.3 us
    all_to_all x1, blocking collectives, shards(): lax.all_to_all(outgoing, 'seq', split_axis=0, concat_axis=0, tiled=True)  89.1 us
    ppermute x8, waiting for transfers between devices, from_behind(): return lax.ppermute(shard, axis, pairs)  48.7 us
    ppermute x8, starting transfers between devices, from_behind(): return lax.ppermute(shard, axis, pairs)  26.5 us
    reduce_scatter x1, waiting for transfers between devices, shards(): lax.psum_scatter(partial_out, 'head', scatter_dimension=0, tiled=True)  19.6 us
    all_to_all x1, starting transfers between devices, _lay_thing(): lax.all_to_all(jnp.stack([u_in for _ in range(lax.axis_size('seq'))], axi...  16.9 us
    all_to_all x1, starting transfers between devices, shards(): lax.all_to_all(cache_blocks, 'seq', split_axis=1, concat_axis=0, tiled=True)  10.7 us
    all_to_all x1, waiting for transfers between devices, shards(): lax.all_to_all(cache_blocks, 'seq', split_axis=1, concat_axis=0, tiled=True)  9.46 us
  transfers between devices with their start and end apart: 14, of which 5 were waited for; matrix products, arithmetic and copies ran while one was open for 9% of the time, Pallas kernels for 0%

profile of v1, /device:TPU:1, one launch (start us, length us, event | category | flops | bytes accessed | tf_op | source)
XLA Modules:
  0.0 395.4 jit_solution(853566011236471502)
XLA Ops:
  8.0 2.7 stack.2
  10.7 16.9 %all-to-all-start = ((bf16[128,768,12]{1,2,0:T(8,128)(2,1)}), bf16[128,768,12]{1,2,0:T(8,128)(2,1)}, u32[]{:S(2)}, u32[]{:S(2)}) async-start(bf16[128,768,12]{1,2,0:T(8,128)(2,1)} %stack.2), calls=%async_computation | async-start | bytes 6291456 | tf_op jit(solution)/shard_map/all_to_all | solution.py:19
  30.2 4.3 %collective-permute-start.5 = (bf16[64,256]{1,0:T(8,128)(2,1)S(1)}, bf16[64,256]{1,0:T(8,128)(2,1)S(1)}, u32[]{:S(2)}, u32[]{:S(2)}) collective-permute-start(bf16[64,256]{1,0:T(8,128)(2,1)S(1)} %copy-done.4), channel_id=1, source_target_pairs={{0,6},{2,8},{4,10},{6,12},{8,14},{10,16},{12,18},{14,20},{16,22},{... | collective-permute-start | bytes 98312 | tf_op jit(solution)/shard_map/ppermute | solution.py:33
  34.5 3.4 collective-permute-start.6
  37.9 2.5 collective-permute-start.7
  40.4 3.1 collective-permute-start
  44.3 47.9 %collective-permute-done.4 = bf16[64,256]{1,0:T(8,128)(2,1)S(1)} collective-permute-done((bf16[64,256]{1,0:T(8,128)(2,1)S(1)}, bf16[64,256]{1,0:T(8,128)(2,1)S(1)}, u32[]{:S(2)}, u32[]{:S(2)}) %collective-permute-start.4) | collective-permute-done | bytes 32800 | tf_op jit(solution)/shard_map/ppermute | solution.py:33
  92.2 2.7 collective-permute-start.1
  94.9 5.7 %collective-permute-start.2 = (bf16[64,256]{1,0:T(8,128)(2,1)S(1)}, bf16[64,256]{1,0:T(8,128)(2,1)S(1)}, u32[]{:S(2)}, u32[]{:S(2)}) collective-permute-start(bf16[64,256]{1,0:T(8,128)(2,1)S(1)} %copy-done.5), channel_id=1, source_target_pairs={{0,4},{2,6},{4,8},{6,10},{8,12},{10,14},{12,16},{14,18},{16,20},{1... | collective-permute-start | bytes 98312 | tf_op jit(solution)/shard_map/ppermute | solution.py:33
  105.2 3.6 reshape.409
  113.2 19.6 %reduce-scatter.2.cloned.1.call-done = f32[32,1536]{1,0:T(8,128)} async-done(((f32[64,1536]{1,0:T(8,128)}), f32[32,1536]{1,0:T(8,128)}) %reduce-scatter.2.cloned.1.call-update) | async-done | bytes 196624 | tf_op jit(solution)/shard_map/reduce_scatter | solution.py:105
  136.8 3.9 scatter_custom_fusion
  140.7 2.5 reshape.413
  143.1 89.1 %all_to_all.27 = bf16[128,1,6,1536]{3,2,1,0:T(8,128)(2,1)} all-to-all(bf16[128,1,6,1536]{3,2,1,0:T(8,128)(2,1)} %bitcast.96), channel_id=1, replica_groups=mesh['seq'=128,'head'=2] {'seq'}, dimensions={0} | all-to-all | bytes 4718592 | tf_op jit(solution)/shard_map/all_to_all | solution.py:131
  232.2 10.7 %all-to-all-start.3 = ((bf16[1,128,8,2,128]{4,3,2,0,1:T(2,128)(2,1)}), bf16[1,128,8,2,128]{4,3,2,0,1:T(2,128)(2,1)S(1)}, u32[]{:S(2)}, u32[]{:S(2)}) async-start(bf16[1,128,8,2,128]{4,3,2,0,1:T(2,128)(2,1)} %bitcast.35), calls=%async_computation.4 | async-start | bytes 1048576 | tf_op jit(solution)/shard_map/all_to_all | solution.py:67
  242.9 3.3 fusion.10
  247.0 3.0 copy.69
  250.0 9.5 %all-to-all-done.3 = bf16[1,128,8,2,128]{4,3,2,0,1:T(2,128)(2,1)S(1)} async-done(((bf16[1,128,8,2,128]{4,3,2,0,1:T(2,128)(2,1)}), bf16[1,128,8,2,128]{4,3,2,0,1:T(2,128)(2,1)S(1)}, u32[]{:S(2)}, u32[]{:S(2)}) %all-to-all-start.3) | async-done | bytes 524320 | tf_op jit(solution)/shard_map/all_to_all | solution.py:67
  259.5 9.1 %all-to-all-start.2 = ((bf16[128,1,6,1536]{3,2,1,0:T(8,128)(2,1)}), bf16[128,1,6,1536]{3,2,1,0:T(8,128)(2,1)}, u32[]{:S(2)}, u32[]{:S(2)}) async-start(bf16[128,1,6,1536]{3,2,1,0:T(8,128)(2,1)} %copy.69), calls=%async_computation.3 | async-start | bytes 6291456 | tf_op jit(solution)/shard_map/all_to_all | solution.py:139
  272.3 5.9 %reshape.464 = bf16[1024,1536]{1,0:T(8,128)(2,1)} reshape(bf16[256,4,1536]{2,1,0:T(4,128)(2,1)} %all-gather.6.cloned.1.call-done) | data formatting | bytes 6291456
  278.2 91.3 %all-gather.4.cloned.1.call-done = bf16[1536,2,1024]{0,1,2:T(2,128)(2,1)} async-done(((bf16[1536,2,4]{0,1,2:T(2,128)(2,1)}), bf16[1536,2,1024]{0,1,2:T(2,128)(2,1)}) %all-gather.4.cloned.1.call-update) | async-done | bytes 6291472 | tf_op jit(solution)/shard_map/all_gather | solution.py:110
  369.5 5.5 %fusion = f32[32,2,1024]{2,0,1:T(8,128)} fusion(bf16[1536,2,1024]{0,1,2:T(2,128)(2,1)} %all-gather.4.cloned.1.call-done, bf16[32,1536]{1,0:T(8,128)(2,1)S(1)} %multiply_convert_fusion), kind=kOutput, calls=%fused_computation.5 | convolution fusion | flops 201326592 | bytes 6651904 | tf_op jit(solution)/shard_map/td,dcf->tcf/dot_general | solution.py:43
  375.0 3.7 reshape.417
  384.6 3.4 fusion.7
  (111 shorter events, 26.1 us)
Async XLA Ops:
  8.0 238.2 %copy-start = (bf16[1,256,1536]{2,1,0:T(8,128)(2,1)S(1)}, bf16[1,256,1536]{2,1,0:T(8,128)(2,1)}, u32[]{:S(2)}) copy-start(bf16[1,256,1536]{2,1,0:T(8,128)(2,1)} %param.27) | copy-start | bytes 2359300
  10.7 17.0 %copy-start.4 = (bf16[64,256]{1,0:T(8,128)(2,1)S(1)}, bf16[64,256]{1,0:T(8,128)(2,1)}, u32[]{:S(2)}) copy-start(bf16[64,256]{1,0:T(8,128)(2,1)} %param.16) | copy-start | bytes 98308
  10.7 29.6 %copy-start.5 = (bf16[64,256]{1,0:T(8,128)(2,1)S(1)}, bf16[64,256]{1,0:T(8,128)(2,1)}, u32[]{:S(2)}) copy-start(bf16[64,256]{1,0:T(8,128)(2,1)} %param.17) | copy-start | bytes 98308
  10.7 32.8 %copy-start.9 = (s32[64]{0:T(128)S(1)}, s32[64]{0:T(128)}, u32[]{:S(2)}) copy-start(s32[64]{0:T(128)} %param.18) | copy-start | bytes 772
  10.7 33.5 %copy-start.2 = (bf16[64,768]{1,0:T(8,128)(2,1)S(1)}, bf16[64,768]{1,0:T(8,128)(2,1)}, u32[]{:S(2)}) copy-start(bf16[64,768]{1,0:T(8,128)(2,1)} %param.15) | copy-start | bytes 294916
  10.7 94.5 %all-to-all-start = ((bf16[128,768,12]{1,2,0:T(8,128)(2,1)}), bf16[128,768,12]{1,2,0:T(8,128)(2,1)}, u32[]{:S(2)}, u32[]{:S(2)}) async-start(bf16[128,768,12]{1,2,0:T(8,128)(2,1)} %stack.2), calls=%async_computation | async-start | bytes 6291456 | tf_op jit(solution)/shard_map/all_to_all | solution.py:19
  27.7 105.1 %reduce-scatter.2.cloned.1.call-start = ((), (), s32[]{:S(2)}) async-start(), calls=%async_computation.5 | async-start | bytes 589824 | tf_op jit(solution)/shard_map/reduce_scatter | solution.py:105
  27.7 64.4 %collective-permute-start.4 = (bf16[64,256]{1,0:T(8,128)(2,1)S(1)}, bf16[64,256]{1,0:T(8,128)(2,1)S(1)}, u32[]{:S(2)}, u32[]{:S(2)}) collective-permute-start(bf16[64,256]{1,0:T(8,128)(2,1)S(1)} %copy-done.4), channel_id=1, source_target_pairs={{0,8},{2,10},{4,12},{6,14},{8,16},{10,18},{12,20},{14,22},{16,24},... | collective-permute-start | bytes 98312 | tf_op jit(solution)/shard_map/ppermute | solution.py:33
  30.2 64.7 %collective-permute-start.5 = (bf16[64,256]{1,0:T(8,128)(2,1)S(1)}, bf16[64,256]{1,0:T(8,128)(2,1)S(1)}, u32[]{:S(2)}, u32[]{:S(2)}) collective-permute-start(bf16[64,256]{1,0:T(8,128)(2,1)S(1)} %copy-done.4), channel_id=1, source_target_pairs={{0,6},{2,8},{4,10},{6,12},{8,14},{10,16},{12,18},{14,20},{16,22},{... | collective-permute-start | bytes 98312 | tf_op jit(solution)/shard_map/ppermute | solution.py:33
  34.5 66.2 %collective-permute-start.6 = (bf16[64,256]{1,0:T(8,128)(2,1)S(1)}, bf16[64,256]{1,0:T(8,128)(2,1)S(1)}, u32[]{:S(2)}, u32[]{:S(2)}) collective-permute-start(bf16[64,256]{1,0:T(8,128)(2,1)S(1)} %copy-done.4), channel_id=1, source_target_pairs={{0,4},{2,6},{4,8},{6,10},{8,12},{10,14},{12,16},{14,18},{16,20},{1... | collective-permute-start | bytes 98312 | tf_op jit(solution)/shard_map/ppermute | solution.py:33
  37.9 65.2 %collective-permute-start.7 = (bf16[64,256]{1,0:T(8,128)(2,1)S(1)}, bf16[64,256]{1,0:T(8,128)(2,1)S(1)}, u32[]{:S(2)}, u32[]{:S(2)}) collective-permute-start(bf16[64,256]{1,0:T(8,128)(2,1)S(1)} %copy-done.4), channel_id=1, source_target_pairs={{0,2},{2,4},{4,6},{6,8},{8,10},{10,12},{12,14},{14,16},{16,18},{18... | collective-permute-start | bytes 98312 | tf_op jit(solution)/shard_map/ppermute | solution.py:33
  40.4 62.7 %collective-permute-start = (bf16[64,256]{1,0:T(8,128)(2,1)S(1)}, bf16[64,256]{1,0:T(8,128)(2,1)S(1)}, u32[]{:S(2)}, u32[]{:S(2)}) collective-permute-start(bf16[64,256]{1,0:T(8,128)(2,1)S(1)} %copy-done.5), channel_id=1, source_target_pairs={{0,8},{2,10},{4,12},{6,14},{8,16},{10,18},{12,20},{14,22},{16,24},... | collective-permute-start | bytes 98312 | tf_op jit(solution)/shard_map/ppermute | solution.py:33
  92.2 11.0 %collective-permute-start.1 = (bf16[64,256]{1,0:T(8,128)(2,1)S(1)}, bf16[64,256]{1,0:T(8,128)(2,1)S(1)}, u32[]{:S(2)}, u32[]{:S(2)}) collective-permute-start(bf16[64,256]{1,0:T(8,128)(2,1)S(1)} %copy-done.5), channel_id=1, source_target_pairs={{0,6},{2,8},{4,10},{6,12},{8,14},{10,16},{12,18},{14,20},{16,22},{... | collective-permute-start | bytes 98312 | tf_op jit(solution)/shard_map/ppermute | solution.py:33
  94.9 8.3 %collective-permute-start.2 = (bf16[64,256]{1,0:T(8,128)(2,1)S(1)}, bf16[64,256]{1,0:T(8,128)(2,1)S(1)}, u32[]{:S(2)}, u32[]{:S(2)}) collective-permute-start(bf16[64,256]{1,0:T(8,128)(2,1)S(1)} %copy-done.5), channel_id=1, source_target_pairs={{0,4},{2,6},{4,8},{6,10},{8,12},{10,14},{12,16},{14,18},{16,20},{1... | collective-permute-start | bytes 98312 | tf_op jit(solution)/shard_map/ppermute | solution.py:33
  100.6 3.4 collective-permute-start.3
  108.9 23.9 %copy-start.1 = (bf16[32,1536]{1,0:T(8,128)(2,1)S(1)}, bf16[32,1536]{1,0:T(8,128)(2,1)}, u32[]{:S(2)}) copy-start(bf16[32,1536]{1,0:T(8,128)(2,1)} %param.20) | copy-start | bytes 294916
  108.9 25.0 %copy-start.8 = (f32[1536]{0:T(1024)S(1)}, f32[1536]{0:T(1024)}, u32[]{:S(2)}) copy-start(f32[1536]{0:T(1024)} %param.21) | copy-start | bytes 18436
  110.5 161.7 %all-gather.6.cloned.1.call-start = ((), (), s32[]{:S(2)}) async-start(), calls=%async_computation.7 | async-start | bytes 3158016 | tf_op jit(solution)/shard_map/all_gather | solution.py:111
  111.1 258.4 %all-gather.4.cloned.1.call-start = ((), (), s32[]{:S(2)}) async-start(), calls=%async_computation.6 | async-start | bytes 6316032 | tf_op jit(solution)/shard_map/all_gather | solution.py:110
  143.1 99.8 %copy-start.10 = (bf16[1,1536,2,256]{3,2,1,0:T(2,128)(2,1)S(1)}, bf16[1,1536,2,256]{3,2,1,0:T(2,128)(2,1)}, u32[]{:S(2)}) copy-start(bf16[1,1536,2,256]{3,2,1,0:T(2,128)(2,1)} %param.26) | copy-start | bytes 4718596
  232.2 27.2 %all-to-all-start.3 = ((bf16[1,128,8,2,128]{4,3,2,0,1:T(2,128)(2,1)}), bf16[1,128,8,2,128]{4,3,2,0,1:T(2,128)(2,1)S(1)}, u32[]{:S(2)}, u32[]{:S(2)}) async-start(bf16[1,128,8,2,128]{4,3,2,0,1:T(2,128)(2,1)} %bitcast.35), calls=%async_computation.4 | async-start | bytes 1048576 | tf_op jit(solution)/shard_map/all_to_all | solution.py:67
  250.0 19.0 %copy-start.3 = (f32[32,6]{0,1:T(8,128)S(1)}, f32[32,6]{0,1:T(8,128)}, u32[]{:S(2)}) copy-start(f32[32,6]{0,1:T(8,128)} %param.23) | copy-start | bytes 2308
  250.0 19.2 %copy-start.11 = (s32[128]{0:T(128)S(1)}, s32[128]{0:T(128)}, u32[]{:S(2)}) copy-start(s32[128]{0:T(128)} %param.29) | copy-start | bytes 1540
  259.5 115.5 %all-to-all-start.2 = ((bf16[128,1,6,1536]{3,2,1,0:T(8,128)(2,1)}), bf16[128,1,6,1536]{3,2,1,0:T(8,128)(2,1)}, u32[]{:S(2)}, u32[]{:S(2)}) async-start(bf16[128,1,6,1536]{3,2,1,0:T(8,128)(2,1)} %copy.69), calls=%async_computation.3 | async-start | bytes 6291456 | tf_op jit(solution)/shard_map/all_to_all | solution.py:139
  (2 other events, 5.2 us)
Sparse Core Ops, SparseCore 0:
  110.6 22.0 reduce-scatter.1
Sparse Core Ops, SparseCore 1:
  115.3 127.9 all-gather.5
  248.2 121.2 all-gather.3
